TPU v7x, 32 devices: a whole 2x2x4 slice. The times are simulated.
32 devices in a mesh: row: 8 (over y, x, core), col: 4 (over z).
Axes of the slice: x: 2, y: 2, z: 4, core: 2. Of those that a mesh axis runs over, the one named last changes fastest.
Arguments:
- left_factors: float32 [128, 256, 32], P(None, ('row', 'col')), may hold values from -12 to 12
- right_factors: float32 [128, 128, 32], P(None, ('col', 'row')), may hold values from -12 to 12
- weight: float32 [1024, 128], replicated, may hold values from -0.1875 to 0.1875
- bias: float32 [128], replicated, may hold values from -2 to 2
- cotangent: float32 [256, 128, 128], P('row', 'col'), may hold values from -6 to 6
Outputs:
- pair_out: float32 [256, 128, 128], P('row', 'col')
- left_grad: float32 [128, 256, 32], P(None, ('row', 'col'))
- right_grad: float32 [128, 128, 32], P(None, ('col', 'row'))
- weight_grad: float32 [1024, 128], replicated
- bias_grad: float32 [128], replicated
All inputs are finite; a program needn't handle non-finite values.
Results may differ from a plain program's by a relative error of at most 0.0001.
Values sent between devices are 32-bit elements; how exact they have to be, the bound alone decides.
A program may use at most 64 MiB of HBM per device.

v0:
```python
import jax
import jax.numpy as jnp
from jax import lax
from jax.sharding import PartitionSpec as P


def per_device(left_factors, right_factors, weight, bias, cotangent):
    high = lax.Precision.HIGHEST
    samples = left_factors.shape[0]
    width = left_factors.shape[2]
    pair_width = weight.shape[1]
    left_all = lax.all_gather(left_factors, "col", axis=1, tiled=True)
    right_all = lax.all_gather(right_factors, "row", axis=1, tiled=True)
    tile_rows = left_all.shape[1]
    tile_cols = right_all.shape[1]
    step_rows = 16
    blocks = tile_rows // step_rows
    left_blocks = left_all.reshape(samples, blocks, step_rows, width).transpose(1, 0, 2, 3)
    cot_blocks = cotangent.reshape(blocks, step_rows, tile_cols, pair_width)

    def visit(carry, item):
        weight_sum, right_sum = carry
        left_block, cot_block = item
        outer = jnp.einsum("sic,sjd->ijcd", left_block, right_all, precision=high) / samples
        flat = outer.reshape(step_rows, tile_cols, width * width)
        pair_block = jnp.einsum("ijk,ke->ije", flat, weight, precision=high) + bias
        grad_flat = jnp.einsum("ije,ke->ijk", cot_block, weight, precision=high)
        weight_sum = weight_sum + jnp.einsum("ijk,ije->ke", flat, cot_block, precision=high)
        grad_outer = grad_flat.reshape(step_rows, tile_cols, width, width)
        left_block_grad = (
            jnp.einsum("ijcd,sjd->sic", grad_outer, right_all, precision=high) / samples
        )
        right_sum = (
            right_sum
            + jnp.einsum("ijcd,sic->sjd", grad_outer, left_block, precision=high) / samples
        )
        return ((weight_sum, right_sum), (pair_block, left_block_grad))

    start = (
        jnp.zeros((width * width, pair_width), jnp.float32),
        jnp.zeros((samples, tile_cols, width), jnp.float32),
    )
    (weight_part, right_part), (pair_blocks, left_pieces) = lax.scan(
        visit, start, (left_blocks, cot_blocks)
    )
    pair_out = pair_blocks.reshape(tile_rows, tile_cols, pair_width)
    left_part = left_pieces.transpose(1, 0, 2, 3).reshape(samples, tile_rows, width)
    bias_part = jnp.sum(cotangent, axis=(0, 1))
    left_total = lax.psum(left_part, "col")
    right_total = lax.psum(right_part, "row")
    left_share = tile_rows // lax.axis_size("col")
    right_share = tile_cols // lax.axis_size("row")
    left_grad = lax.dynamic_slice_in_dim(
        left_total, lax.axis_index("col") * left_share, left_share, 1
    )
    right_grad = lax.dynamic_slice_in_dim(
        right_total, lax.axis_index("row") * right_share, right_share, 1
    )
    weight_half, bias_half = lax.psum((weight_part, bias_part), "col")
    weight_total, bias_total = lax.psum((weight_half, bias_half), "row")
    total_rows = tile_rows * lax.axis_size("row")
    weight_grad = weight_total / total_rows
    bias_grad = bias_total / total_rows
    return (pair_out, left_grad, right_grad, weight_grad, bias_grad)


def solution(mesh):
    in_specs = (
        P(None, ("row", "col"), None),
        P(None, ("col", "row"), None),
        P(),
        P(),
        P("row", "col", None),
    )
    out_specs = (
        P("row", "col", None),
        P(None, ("row", "col"), None),
        P(None, ("col", "row"), None),
        P(),
        P(),
    )
    return jax.shard_map(
        per_device, mesh=mesh, in_specs=in_specs, out_specs=out_specs, check_vma=False
    )
```

profile of v0, /device:TPU:0, one launch (start us, length us, event | category | flops | bytes accessed | tf_op | source)
XLA Modules:
  0.0 329.0 jit_solution(1549016555022079670)
XLA Ops:
  7.2 0.0 all-reduce.7.cloned.1.call-start
  7.2 11.6 %all_gather.7 = f32[128,32,32]{0,2,1:T(8,128)S(1)} all-gather(f32[128,4,32]{0,2,1:T(8,128)} %param.8), channel_id=1, replica_groups=mesh['row'=8,'col'=4] {'row'}, dimensions={1}, use_global_device_ids=true | all-gather | bytes 589824 | tf_op jit(solution)/shard_map/all_gather | solution.py:13
  18.9 0.3 copy.17
  19.2 16.6 %all_gather.6 = f32[128,32,32]{0,2,1:T(8,128)S(1)} all-gather(f32[128,8,32]{0,2,1:T(8,128)} %param.7), channel_id=1, replica_groups=mesh['row'=8,'col'=4] {'col'}, dimensions={1}, use_global_device_ids=true | all-gather | bytes 655360 | tf_op jit(solution)/shard_map/all_gather | solution.py:12
  35.7 170.8 %while.17 = (s32[]{:T(128)}, f32[1024,128]{1,0:T(8,128)}, f32[128,32,32]{0,2,1:T(8,128)}, f32[2,16,32,128]{3,2,1,0:T(8,128)}, f32[2,128,16,32]{1,3,2,0:T(8,128)}...) while((s32[]{:T(128)}, f32[1024,128]{1,0:T(8,128)}, ...), condition=%wide.region_1.2_spmd.clone, body=%wide.region_0.1_spmd.clone.sunk | while | flops 4833148928 | bytes 49812356 | solution.py:43
  59.1 0.0 copy-start.2
  59.1 0.8 copy-done.2
  59.9 9.1 %multiply_bitcast_fusion.2 = f32[16,32,32,32]{3,2,1,0:T(8,128)} fusion(f32[128,32,32]{0,1,2:T(8,128)S(1)} %get-tuple-element.222, f32[2,128,16,32]{1,3,2,0:T(8,128)S(1)} %get-tuple-element.221, s32[]{:T(128)} %get-tuple-element.204), kind=kOutput, calls=%fused_computation.2.clone.1 | convolution fusion | flops 805830656 | bytes 2883588 | tf_op jit(solution)/shard_map/while/body/eval_jaxpr/sic,sjd->ijcd/dot_general | solution.py:24
  68.9 0.0 copy-start.1
  68.9 6.7 %reshape.43 = f32[16,32,1024]{2,1,0:T(8,128)S(1)} reshape(f32[16,32,32,32]{3,2,1,0:T(8,128)} %multiply_bitcast_fusion.2) | data formatting | bytes 4194304 | tf_op jit(solution)/shard_map/while/body/eval_jaxpr/reshape | solution.py:25
  75.6 0.0 copy-start.4
  75.7 5.2 %fusion.67 = f32[1024,128]{1,0:T(8,128)} fusion(f32[16,32,1024]{2,1,0:T(8,128)S(1)} %reshape.43, f32[1024,128]{1,0:T(8,128)} %get-tuple-element.205, pred[]{:T(512)S(6)} %compare.3, f32[2,16,32,128]{3,2,1,0:T(8,128)} %get-tuple-element.223, s32[]{:T(128)} %get-tuple-element.204), kind=kOutput, calls=%fused_computation.5.clone.1 | convolution fusion | flops 805568512 | bytes 3408385 | tf_op jit(solution)/shard_map/while/body/eval_jaxpr/ijk,ije->ke/dot_general | solution.py:28
  80.9 0.0 copy-done.1
  80.9 0.0 copy-start.8
  80.9 7.7 %fusion.68 = f32[16,32,32,32]{3,1,2,0:T(8,128)S(1)} fusion(f32[32,32,128,1]{2,1,0,3:T(8,128)S(1)} %bitcast.110, f32[2,16,32,128]{3,2,1,0:T(8,128)} %get-tuple-element.223, s32[]{:T(128)} %get-tuple-element.204), kind=kOutput, calls=%fused_computation.19.clone.1 | convolution fusion | flops 805306368 | bytes 2884096 | tf_op jit(solution)/shard_map/while/body/eval_jaxpr/ije,ke->ijk/dot_general | solution.py:27
  88.6 0.0 copy-start
  88.6 3.2 copy-done
  91.8 0.0 copy-done.4
  91.8 17.0 %fusion.69 = f32[128,32,32]{0,2,1:T(8,128)S(1)} fusion(f32[16,32,32,32]{3,1,2,0:T(8,128)S(1)} %fusion.68, f32[128,32,32]{0,2,1:T(8,128)S(1)} %copy-done.4, pred[]{:T(512)S(6)} %compare.3, f32[2,128,16,32]{1,3,2,0:T(8,128)} %copy-done.2, s32[]{:T(128)} %get-tuple-element.204), kind=kOutput, calls=%fused_computation.7.clone.1 | convolution fusion | flops 805699584 | bytes 3408385 | tf_op jit(solution)/shard_map/while/body/eval_jaxpr/ijcd,sic->sjd/dot_general | solution.py:35
  108.8 0.0 copy-start.5
  108.8 0.8 copy-done.5
  109.5 0.0 copy-done.8
  109.6 2.5 fusion.70
  112.1 0.0 copy-start.6
  112.1 10.6 %copy.39 = f32[16,32,32,32]{1,2,3,0:T(8,128)} copy(f32[16,32,32,32]{3,1,2,0:T(8,128)} %copy-done) | data formatting | bytes 4194304 | tf_op jit(solution)/shard_map/while/body/eval_jaxpr/ije,ke->ijk/dot_general | solution.py:27
  122.7 0.0 copy-start.3
  122.7 0.0 copy-done.6
  122.7 9.2 %fusion.71 = f32[2,128,16,32]{1,3,2,0:T(8,128)S(1)} fusion(f32[2,128,16,32]{1,3,2,0:T(8,128)S(1)} %copy-done.6, s32[]{:T(128)} %get-tuple-element.204, f32[16,32,32,32]{1,2,3,0:T(8,128)} %copy.39, f32[128,32,32]{0,1,2:T(8,128)S(1)} %get-tuple-element.222), kind=kOutput, calls=%fused_computation.14.clone.1 | convolution fusion | flops 805371904 | bytes 2883588 | tf_op jit(solution)/shard_map/while/body/eval_jaxpr/ijcd,sjd->sic/dot_general | solution.py:31
  131.9 0.0 copy-start.7
  131.9 0.8 copy-done.7
  132.7 0.0 copy-done.3
  132.7 0.8 copy-done.2
  133.5 9.0 %multiply_bitcast_fusion.2 = f32[16,32,32,32]{3,2,1,0:T(8,128)} fusion(f32[128,32,32]{0,1,2:T(8,128)S(1)} %get-tuple-element.222, f32[2,128,16,32]{1,3,2,0:T(8,128)S(1)} %get-tuple-element.221, s32[]{:T(128)} %get-tuple-element.204), kind=kOutput, calls=%fused_computation.2.clone.1 | convolution fusion | flops 805830656 | bytes 2883588 | tf_op jit(solution)/shard_map/while/body/eval_jaxpr/sic,sjd->ijcd/dot_general | solution.py:24
  142.6 6.7 %reshape.43 = f32[16,32,1024]{2,1,0:T(8,128)S(1)} reshape(f32[16,32,32,32]{3,2,1,0:T(8,128)} %multiply_bitcast_fusion.2) | data formatting | bytes 4194304 | tf_op jit(solution)/shard_map/while/body/eval_jaxpr/reshape | solution.py:25
  149.3 0.0 copy-start.4
  149.3 5.4 %fusion.67 = f32[1024,128]{1,0:T(8,128)} fusion(f32[16,32,1024]{2,1,0:T(8,128)S(1)} %reshape.43, f32[1024,128]{1,0:T(8,128)} %get-tuple-element.205, pred[]{:T(512)S(6)} %compare.3, f32[2,16,32,128]{3,2,1,0:T(8,128)} %get-tuple-element.223, s32[]{:T(128)} %get-tuple-element.204), kind=kOutput, calls=%fused_computation.5.clone.1 | convolution fusion | flops 805568512 | bytes 3408385 | tf_op jit(solution)/shard_map/while/body/eval_jaxpr/ijk,ije->ke/dot_general | solution.py:28
  154.7 0.0 copy-done.1
  154.7 7.7 %fusion.68 = f32[16,32,32,32]{3,1,2,0:T(8,128)S(1)} fusion(f32[32,32,128,1]{2,1,0,3:T(8,128)S(1)} %bitcast.110, f32[2,16,32,128]{3,2,1,0:T(8,128)} %get-tuple-element.223, s32[]{:T(128)} %get-tuple-element.204), kind=kOutput, calls=%fused_computation.19.clone.1 | convolution fusion | flops 805306368 | bytes 2884096 | tf_op jit(solution)/shard_map/while/body/eval_jaxpr/ije,ke->ijk/dot_general | solution.py:27
  162.4 0.0 copy-start
  162.4 3.2 copy-done
  165.6 0.0 copy-done.4
  165.6 17.0 %fusion.69 = f32[128,32,32]{0,2,1:T(8,128)S(1)} fusion(f32[16,32,32,32]{3,1,2,0:T(8,128)S(1)} %fusion.68, f32[128,32,32]{0,2,1:T(8,128)S(1)} %copy-done.4, pred[]{:T(512)S(6)} %compare.3, f32[2,128,16,32]{1,3,2,0:T(8,128)} %copy-done.2, s32[]{:T(128)} %get-tuple-element.204), kind=kOutput, calls=%fused_computation.7.clone.1 | convolution fusion | flops 805699584 | bytes 3408385 | tf_op jit(solution)/shard_map/while/body/eval_jaxpr/ijcd,sic->sjd/dot_general | solution.py:35
  182.6 0.0 copy-start.5
  182.6 0.8 copy-done.5
  183.4 0.0 copy-done.8
  183.4 2.5 fusion.70
  185.9 10.6 %copy.39 = f32[16,32,32,32]{1,2,3,0:T(8,128)} copy(f32[16,32,32,32]{3,1,2,0:T(8,128)} %copy-done) | data formatting | bytes 4194304 | tf_op jit(solution)/shard_map/while/body/eval_jaxpr/ije,ke->ijk/dot_general | solution.py:27
  196.5 0.0 copy-done.6
  196.5 9.2 %fusion.71 = f32[2,128,16,32]{1,3,2,0:T(8,128)S(1)} fusion(f32[2,128,16,32]{1,3,2,0:T(8,128)S(1)} %copy-done.6, s32[]{:T(128)} %get-tuple-element.204, f32[16,32,32,32]{1,2,3,0:T(8,128)} %copy.39, f32[128,32,32]{0,1,2:T(8,128)S(1)} %get-tuple-element.222), kind=kOutput, calls=%fused_computation.14.clone.1 | convolution fusion | flops 805371904 | bytes 2883588 | tf_op jit(solution)/shard_map/while/body/eval_jaxpr/ijcd,sjd->sic/dot_general | solution.py:31
  205.7 0.0 copy-start.7
  205.7 0.8 copy-done.7
  206.5 0.0 copy-done.3
  206.5 0.0 all-reduce.7.cloned.1.call-update
  206.6 0.0 all-reduce.5.cloned.1.call-start
  206.6 52.6 %all-reduce.7.cloned.1.call-done = (f32[128,32,32]{0,2,1:T(8,128)}, f32[1024,128]{1,0:T(8,128)}) async-done(((f32[128,32,32]{0,2,1:T(8,128)}, f32[1024,128]{1,0:T(8,128)}), (f32[128,32,32]{0,2,1:T(8,128)}, f32[1024,128]{1,0:T(8,128)})) %all-reduce.7.cloned.1.call-update) | async-done | bytes 1048592 | tf_op jit(solution)/shard_map/psum | solution.py:49
  259.2 0.0 all-reduce.5.cloned.1.call-update
  259.2 1.2 reduce_sum.9
  260.4 10.0 %psum.46 = f32[128]{0:T(128)S(1)} all-reduce(f32[128]{0:T(128)S(1)} %reduce_sum.9), channel_id=1, replica_groups=mesh['row'=8,'col'=4] {'col'}, use_global_device_ids=true, to_apply=%region_7.8 | all-reduce | flops 128 | bytes 1024 | tf_op jit(solution)/shard_map/psum | solution.py:59
  270.4 11.8 %psum.47 = f32[128]{0:T(128)S(1)} all-reduce(f32[128]{0:T(128)S(1)} %psum.46), channel_id=1, replica_groups=mesh['row'=8,'col'=4] {'row'}, use_global_device_ids=true, to_apply=%region_8.9 | all-reduce | flops 128 | bytes 1024 | tf_op jit(solution)/shard_map/psum | solution.py:60
  282.3 0.5 broadcast_multiply_fusion.1
  282.8 1.6 constant_dynamic-slice_fusion.1
  284.4 34.1 %all-reduce.5.cloned.1.call-done = (f32[128,32,32]{0,2,1:T(8,128)}, f32[1024,128]{1,0:T(8,128)}) async-done(((f32[128,32,32]{0,2,1:T(8,128)}, f32[1024,128]{1,0:T(8,128)}), (f32[128,32,32]{0,2,1:T(8,128)}, f32[1024,128]{1,0:T(8,128)})) %all-reduce.5.cloned.1.call-update) | async-done | bytes 1048592 | tf_op jit(solution)/shard_map/psum | solution.py:50
  318.5 1.9 broadcast_multiply_fusion
  320.3 1.5 constant_dynamic-slice_fusion
  (9 shorter events, 0.0 us)
Async XLA Ops:
  7.2 252.0 %all-reduce.7.cloned.1.call-start = ((), (), s32[]{:S(2)}) async-start(), calls=%async_computation.1 | async-start | bytes 2097152 | tf_op jit(solution)/shard_map/psum | solution.py:49
  59.1 0.8 copy-start.2
  68.9 12.0 %copy-start.1 = (f32[1024,128]{1,0:T(8,128)S(1)}, f32[1024,128]{1,0:T(8,128)}, u32[]{:S(2)}) copy-start(f32[1024,128]{1,0:T(8,128)} %get-tuple-element.224) | copy-start | bytes 1572868 | tf_op jit(solution)/shard_map/while
  75.6 16.1 %copy-start.4 = (f32[128,32,32]{0,2,1:T(8,128)S(1)}, f32[128,32,32]{0,2,1:T(8,128)}, u32[]{:S(2)}) copy-start(f32[128,32,32]{0,2,1:T(8,128)} %get-tuple-element.206) | copy-start | bytes 1572868 | tf_op jit(solution)/shard_map/while
  80.9 28.7 %copy-start.8 = (f32[128]{0:T(128)S(1)}, f32[128]{0:T(128)}, u32[]{:S(2)}) copy-start(f32[128]{0:T(128)} %get-tuple-element.225) | copy-start | bytes 1540 | tf_op jit(solution)/shard_map/while
  88.6 3.2 copy-start
  108.8 0.8 copy-start.5
  112.1 10.6 %copy-start.6 = (f32[2,128,16,32]{1,3,2,0:T(8,128)S(1)}, f32[2,128,16,32]{1,3,2,0:T(8,128)}, u32[]{:S(2)}) copy-start(f32[2,128,16,32]{1,3,2,0:T(8,128)} %get-tuple-element.208) | copy-start | bytes 1572868 | tf_op jit(solution)/shard_map/while
  122.7 10.0 %copy-start.3 = (f32[2,128,16,32]{1,3,2,0:T(8,128)S(1)}, f32[2,128,16,32]{1,3,2,0:T(8,128)}, u32[]{:S(2)}) copy-start(f32[2,128,16,32]{1,3,2,0:T(8,128)} %copy-done.2) | copy-start | bytes 1572868 | tf_op jit(solution)/shard_map/while
  131.9 0.8 copy-start.7
  132.7 0.8 copy-start.2
  142.6 12.1 %copy-start.1 = (f32[1024,128]{1,0:T(8,128)S(1)}, f32[1024,128]{1,0:T(8,128)}, u32[]{:S(2)}) copy-start(f32[1024,128]{1,0:T(8,128)} %get-tuple-element.224) | copy-start | bytes 1572868 | tf_op jit(solution)/shard_map/while
  149.3 16.3 %copy-start.4 = (f32[128,32,32]{0,2,1:T(8,128)S(1)}, f32[128,32,32]{0,2,1:T(8,128)}, u32[]{:S(2)}) copy-start(f32[128,32,32]{0,2,1:T(8,128)} %get-tuple-element.206) | copy-start | bytes 1572868 | tf_op jit(solution)/shard_map/while
  154.7 28.7 %copy-start.8 = (f32[128]{0:T(128)S(1)}, f32[128]{0:T(128)}, u32[]{:S(2)}) copy-start(f32[128]{0:T(128)} %get-tuple-element.225) | copy-start | bytes 1540 | tf_op jit(solution)/shard_map/while
  162.4 3.2 copy-start
  182.6 0.8 copy-start.5
  185.9 10.6 %copy-start.6 = (f32[2,128,16,32]{1,3,2,0:T(8,128)S(1)}, f32[2,128,16,32]{1,3,2,0:T(8,128)}, u32[]{:S(2)}) copy-start(f32[2,128,16,32]{1,3,2,0:T(8,128)} %get-tuple-element.208) | copy-start | bytes 1572868 | tf_op jit(solution)/shard_map/while
  196.5 10.0 %copy-start.3 = (f32[2,128,16,32]{1,3,2,0:T(8,128)S(1)}, f32[2,128,16,32]{1,3,2,0:T(8,128)}, u32[]{:S(2)}) copy-start(f32[2,128,16,32]{1,3,2,0:T(8,128)} %copy-done.2) | copy-start | bytes 1572868 | tf_op jit(solution)/shard_map/while
  205.7 0.8 copy-start.7
  206.6 111.9 %all-reduce.5.cloned.1.call-start = ((), (), s32[]{:S(2)}) async-start(), calls=%async_computation | async-start | bytes 2097152 | tf_op jit(solution)/shard_map/psum | solution.py:50
Sparse Core Ops, SparseCore 0:
  206.7 52.4 all-reduce.6
  262.4 56.0 all-reduce.4
where the time goes:
time: 332 us; the launch traced here: 329 us
  matrix products  101 us (30%)
  waiting for transfers between devices  86.7 us (26%)
  blocking collectives  50 us (15%)
  local copies, waits for them, and re-layouts  49.2 us (15%)
  loops' own time  23.5 us (7%)
  between operations  14.5 us (4%)
  other arithmetic  3.58 us (1%)
    psum x1, waiting for transfers between devices, per_device(): left_total = lax.psum(left_part, 'col')  52.6 us
    psum x1, waiting for transfers between devices, per_device(): right_total = lax.psum(right_part, 'row')  34.1 us
    dot_general x2, matrix products, visit(): jnp.einsum('ijcd,sic->sjd', grad_outer, left_block, precision=high)  33.9 us
    another operation x1, loops' own time, per_device(): lax.scan(visit, start, (left_blocks, cot_blocks))  23.5 us
    dot_general x2, local copies, waits for them, and re-layouts, visit(): grad_flat = jnp.einsum('ije,ke->ijk', cot_block, weight, precision=high)  21.3 us
    dot_general x2, matrix products, visit(): jnp.einsum('ijcd,sjd->sic', grad_outer, right_all, precision=high) / samples  18.4 us
    dot_general x2, matrix products, visit(): jnp.einsum('sic,sjd->ijcd', left_block, right_all, precision=high) / samples  18.1 us
    all_gather x1, blocking collectives, per_device(): left_all = lax.all_gather(left_factors, 'col', axis=1, tiled=True)  16.6 us
  transfers between devices with their start and end apart: 2, of which 2 were waited for; matrix products, arithmetic and copies ran while one was open for 1% of the time, Pallas kernels for 0%

commit v1 on v0

v1 whole, which is shorter than its diff:
```python
import functools

import jax
import jax.numpy as jnp
from jax import lax
from jax.experimental import pallas as pl
from jax.experimental.pallas import tpu as pltpu
from jax.sharding import PartitionSpec as P

F32 = jnp.float32
BF16 = jnp.bfloat16
MESH = pl.DeviceIdType.MESH
VMEM = pl.BlockSpec(memory_space=pltpu.VMEM)
ROWS_PER_STEP = 8


def split(x):
    high = x.astype(BF16)
    return high, (x - high.astype(F32)).astype(BF16)


def dot(a, b):
    return lax.dot_general(a, b, (((1,), (0,)), ((), ())), preferred_element_type=F32)


def dot3(a_high, a_low, b_high, b_low):
    return dot(a_high, b_high) + (dot(a_high, b_low) + dot(a_low, b_high))


def swap_groups(pieces):
    lane = lax.broadcasted_iota(jnp.int32, pieces[0].shape, 1)
    low = lane < 64
    even = (lane & 32) == 0

    def far(a, b):
        moved = pltpu.roll(jnp.where(low, b, a), 64, 1)
        return jnp.where(low, a, moved), jnp.where(low, moved, b)

    def near(a, b):
        return (
            jnp.where(even, a, pltpu.roll(b, 32, 1)),
            jnp.where(even, pltpu.roll(a, 96, 1), b),
        )

    p0, p2 = far(pieces[0], pieces[2])
    p1, p3 = far(pieces[1], pieces[3])
    p0, p1 = near(p0, p1)
    p2, p3 = near(p2, p3)
    return p0, p1, p2, p3


def gather_kernel(nrow, ncol, l_ref, r_ref, lo_ref, ro_ref, ls, lr, rs, rr):
    row, col = lax.axis_index("row"), lax.axis_index("col")
    barrier = pltpu.get_barrier_semaphore()

    @pl.loop(1, ncol)
    def _(k):
        pl.semaphore_signal(
            barrier, inc=1, device_id={"row": row, "col": lax.rem(col + k, ncol)}, device_id_type=MESH
        )

    @pl.loop(1, nrow)
    def _(k):
        pl.semaphore_signal(
            barrier, inc=1, device_id={"row": lax.rem(row + k, nrow), "col": col}, device_id_type=MESH
        )

    pl.semaphore_wait(barrier, nrow + ncol - 2)

    def left_copy(k):
        return pltpu.make_async_remote_copy(
            src_ref=l_ref, dst_ref=lo_ref.at[col], send_sem=ls.at[k], recv_sem=lr.at[k],
            device_id={"row": row, "col": lax.rem(col + k, ncol)}, device_id_type=MESH,
        )

    def right_copy(k):
        return pltpu.make_async_remote_copy(
            src_ref=r_ref, dst_ref=ro_ref.at[row], send_sem=rs.at[k], recv_sem=rr.at[k],
            device_id={"row": lax.rem(row + k, nrow), "col": col}, device_id_type=MESH,
        )

    @pl.loop(1, ncol)
    def _(k):
        left_copy(k).start()

    @pl.loop(1, nrow)
    def _(k):
        right_copy(k).start()

    lo_ref[col] = l_ref[...]
    ro_ref[row] = r_ref[...]

    @pl.loop(1, ncol)
    def _(k):
        left_copy(k).wait()

    @pl.loop(1, nrow)
    def _(k):
        right_copy(k).wait()


def compute_kernel(
    width, lo_ref, ro_ref, w_ref, b_ref, cot_ref,
    pair_ref, lp_ref, rp_ref, wp_ref,
    l_h, l_l, lt_h, lt_l, r_h, r_l, rt_h, rt_l, w_h, w_l, wt_h, wt_l,
    rows_scr, out_scr, t_h, t_l, h_h, h_l, wsum, rsum, lsum,
):
    ncol, samples, lw = lo_ref.shape
    nrow, _, rw = ro_ref.shape
    tile_rows, tile_cols = ncol * lw // width, nrow * rw // width
    channels = width * width
    scale = 1.0 / samples
    per = 128 // width

    for k in range(ncol):
        lsum[:, k * lw : (k + 1) * lw] = lo_ref[k]
    left = lsum[...]
    l_h[...], l_l[...] = split(left)
    lt_h[...], lt_l[...] = split(left.T)
    for k in range(nrow):
        rows_scr[k * rw : (k + 1) * rw, :] = ro_ref[k].T
    for d in range(width):
        rsum[d * tile_cols : (d + 1) * tile_cols, :] = rows_scr[pl.ds(d, tile_cols, stride=width), :]
    right = rsum[...]
    rt_h[...], rt_l[...] = split(right)
    r_h[...], r_l[...] = split(right.T)
    for d in range(width):
        rows_scr[d * width : (d + 1) * width, :] = w_ref[pl.ds(d, width, stride=width), :]
    weight = rows_scr[0:channels, :]
    w_h[...], w_l[...] = split(weight)
    wt_h[...], wt_l[...] = split(weight.T)

    wsum[...] = jnp.zeros_like(wsum)
    rsum[...] = jnp.zeros_like(rsum)
    step_lanes = ROWS_PER_STEP * width
    step_rows = ROWS_PER_STEP * tile_cols
    halves = step_lanes // 128

    def step(g, bias_sum):
        lanes = pl.ds(pl.multiple_of(g * step_lanes, step_lanes), step_lanes)
        rows = pl.ds(pl.multiple_of(g * step_rows, step_rows), step_rows)
        cot = cot_ref[rows, :]
        cot_h, cot_l = split(cot)
        cott_h, cott_l = split(cot.T)
        out_scr[...] = dot3(rt_h[...], rt_l[...], l_h[:, lanes], l_l[:, lanes]) * scale
        for block in range(width // per):
            for half in range(halves):
                pieces = [
                    out_scr[(block * per + a) * tile_cols : (block * per + a + 1) * tile_cols,
                            half * 128 : (half + 1) * 128]
                    for a in range(per)
                ]
                for a, piece in enumerate(swap_groups(pieces)):
                    at = (half * per + a) * tile_cols
                    high, low = split(piece)
                    t_h[at : at + tile_cols, block * 128 : (block + 1) * 128] = high
                    t_l[at : at + tile_cols, block * 128 : (block + 1) * 128] = low
        pair_ref[rows, :] = dot3(t_h[...], t_l[...], w_h[...], w_l[...]) + b_ref[...]
        wsum[...] += dot3(cott_h, cott_l, t_h[...], t_l[...])
        grad = dot3(cot_h, cot_l, wt_h[...], wt_l[...]) * scale
        for block in range(width // per):
            for half in range(halves):
                pieces = [
                    grad[(half * per + a) * tile_cols : (half * per + a + 1) * tile_cols,
                         block * 128 : (block + 1) * 128]
                    for a in range(per)
                ]
                for a, piece in enumerate(swap_groups(pieces)):
                    at = (block * per + a) * tile_cols
                    high, low = split(piece)
                    h_h[at : at + tile_cols, half * 128 : (half + 1) * 128] = high
                    h_l[at : at + tile_cols, half * 128 : (half + 1) * 128] = low
        lsum[:, lanes] = dot3(r_h[...], r_l[...], h_h[...], h_l[...])
        rsum[...] += dot3(h_h[...], h_l[...], lt_h[lanes, :], lt_l[lanes, :])
        return bias_sum + jnp.sum(cot, axis=0, keepdims=True)

    bias_sum = lax.fori_loop(
        0, tile_rows // ROWS_PER_STEP, step, jnp.zeros((1, cot_ref.shape[1]), F32)
    )

    for k in range(ncol):
        lp_ref[k] = lsum[:, k * lw : (k + 1) * lw]
    for d in range(width):
        rows_scr[pl.ds(d, tile_cols, stride=width), :] = rsum[d * tile_cols : (d + 1) * tile_cols, :]
    for k in range(nrow):
        rp_ref[k] = rows_scr[k * rw : (k + 1) * rw, :].T
    turned = wsum[...].T
    for d in range(width):
        rows_scr[pl.ds(d, width, stride=width), :] = turned[d * width : (d + 1) * width, :]
    devices, chunk, cols = wp_ref.shape
    share = channels // devices
    tail = jnp.broadcast_to(bias_sum, (8, cols))
    for q in range(devices):
        wp_ref[q, 0:share, :] = rows_scr[q * share : (q + 1) * share, :]
        wp_ref[q, share:chunk, :] = tail


def reduce_kernel(
    nrow, ncol, total_rows, lp_ref, rp_ref, wp_ref, lg_ref, rg_ref, wg_ref, bg_ref,
    lbuf, rbuf, wbuf, ls, lr, rs, rr, ws, wr, gs, gr,
):
    row, col = lax.axis_index("row"), lax.axis_index("col")
    n = nrow * ncol
    me = row * ncol + col
    share = wg_ref.shape[1]

    def device(k):
        p = lax.rem(me + k, n)
        return {"row": p // ncol, "col": lax.rem(p, ncol)}

    barrier = pltpu.get_barrier_semaphore()

    @pl.loop(1, n)
    def _(k):
        pl.semaphore_signal(barrier, inc=1, device_id=device(k), device_id_type=MESH)

    pl.semaphore_wait(barrier, n - 1)

    def weight_copy(k):
        return pltpu.make_async_remote_copy(
            src_ref=wp_ref.at[lax.rem(me + k, n)], dst_ref=wbuf.at[me],
            send_sem=ws.at[k], recv_sem=wr.at[k], device_id=device(k), device_id_type=MESH,
        )

    def whole_copy(k):
        return pltpu.make_async_remote_copy(
            src_ref=wg_ref.at[me], dst_ref=wg_ref.at[me],
            send_sem=gs.at[k], recv_sem=gr.at[k], device_id=device(k), device_id_type=MESH,
        )

    def left_copy(k):
        peer = lax.rem(col + k, ncol)
        return pltpu.make_async_remote_copy(
            src_ref=lp_ref.at[peer], dst_ref=lbuf.at[col], send_sem=ls.at[k], recv_sem=lr.at[k],
            device_id={"row": row, "col": peer}, device_id_type=MESH,
        )

    def right_copy(k):
        peer = lax.rem(row + k, nrow)
        return pltpu.make_async_remote_copy(
            src_ref=rp_ref.at[peer], dst_ref=rbuf.at[row], send_sem=rs.at[k], recv_sem=rr.at[k],
            device_id={"row": peer, "col": col}, device_id_type=MESH,
        )

    def each(count, act):
        pl.loop(1, count)(act)

    each(n, lambda k: weight_copy(k).start())
    each(ncol, lambda k: left_copy(k).start())
    each(nrow, lambda k: right_copy(k).start())
    wbuf[me] = wp_ref[me]
    lbuf[col] = lp_ref[col]
    rbuf[row] = rp_ref[row]
    each(n, lambda k: weight_copy(k).wait())
    total = lax.fori_loop(1, n, lambda q, acc: acc + wbuf[q], wbuf[0]) / total_rows
    wg_ref[me] = total[0:share, :]
    bg_ref[...] = total[share : share + 1, :]
    each(n, lambda k: whole_copy(k).start())
    each(ncol, lambda k: left_copy(k).wait())
    lg_ref[...] = functools.reduce(lambda a, b: a + b, [lbuf[q] for q in range(ncol)])
    each(nrow, lambda k: right_copy(k).wait())
    rg_ref[...] = functools.reduce(lambda a, b: a + b, [rbuf[q] for q in range(nrow)])
    each(n, lambda k: whole_copy(k).wait())


def per_device(nrow, ncol, left_factors, right_factors, weight, bias, cotangent):
    samples, li, width = left_factors.shape
    rj = right_factors.shape[1]
    tile_rows, tile_cols, pair_width = cotangent.shape
    channels = weight.shape[0]
    n = nrow * ncol
    lw, rw = li * width, rj * width
    share = channels // n
    dma = pltpu.SemaphoreType.DMA

    def shape(*dims):
        return jax.ShapeDtypeStruct(dims, F32)

    lo, ro = pl.pallas_call(
        functools.partial(gather_kernel, nrow, ncol),
        out_shape=(shape(ncol, samples, lw), shape(nrow, samples, rw)),
        in_specs=[VMEM] * 2,
        out_specs=[VMEM] * 2,
        scratch_shapes=[dma((ncol,)), dma((ncol,)), dma((nrow,)), dma((nrow,))],
        compiler_params=pltpu.CompilerParams(collective_id=0, has_side_effects=True),
        name="gather",
    )(left_factors.reshape(samples, lw), right_factors.reshape(samples, rw))

    lanes, rows = tile_rows * width, tile_cols * width
    big = max(rows, channels)
    step_lanes, step_rows = ROWS_PER_STEP * width, ROWS_PER_STEP * tile_cols
    scratch = [
        pltpu.VMEM(dims, dtype)
        for dims, dtype in [
            ((samples, lanes), BF16), ((samples, lanes), BF16),
            ((lanes, samples), BF16), ((lanes, samples), BF16),
            ((samples, rows), BF16), ((samples, rows), BF16),
            ((rows, samples), BF16), ((rows, samples), BF16),
            ((channels, pair_width), BF16), ((channels, pair_width), BF16),
            ((pair_width, channels), BF16), ((pair_width, channels), BF16),
            ((big, 128), F32), ((rows, step_lanes), F32),
            ((step_rows, channels), BF16), ((step_rows, channels), BF16),
            ((rows, step_lanes), BF16), ((rows, step_lanes), BF16),
            ((pair_width, channels), F32), ((rows, samples), F32), ((samples, lanes), F32),
        ]
    ]
    pair, lp, rp, wp = pl.pallas_call(
        functools.partial(compute_kernel, width),
        out_shape=(
            shape(tile_rows * tile_cols, pair_width),
            shape(ncol, samples, lw),
            shape(nrow, samples, rw),
            shape(n, share + 8, pair_width),
        ),
        in_specs=[VMEM] * 5,
        out_specs=[VMEM] * 4,
        scratch_shapes=scratch,
        name="tile",
    )(lo, ro, weight, bias.reshape(1, pair_width), cotangent.reshape(tile_rows * tile_cols, pair_width))

    lg, rg, wg, bg = pl.pallas_call(
        functools.partial(reduce_kernel, nrow, ncol, tile_rows * nrow),
        out_shape=(
            shape(samples, lw), shape(samples, rw), shape(n, share, pair_width), shape(1, pair_width),
        ),
        in_specs=[VMEM] * 3,
        out_specs=[VMEM] * 4,
        scratch_shapes=[
            pltpu.VMEM((ncol, samples, lw), F32),
            pltpu.VMEM((nrow, samples, rw), F32),
            pltpu.VMEM((n, share + 8, pair_width), F32),
            dma((ncol,)), dma((ncol,)), dma((nrow,)), dma((nrow,)),
            dma((n,)), dma((n,)), dma((n,)), dma((n,)),
        ],
        compiler_params=pltpu.CompilerParams(collective_id=1, has_side_effects=True),
        name="reduce",
    )(lp, rp, wp)
    return (
        pair.reshape(tile_rows, tile_cols, pair_width),
        lg.reshape(samples, li, width),
        rg.reshape(samples, rj, width),
        wg.reshape(channels, pair_width),
        bg.reshape(pair_width),
    )


def solution(mesh):
    nrow, ncol = mesh.shape["row"], mesh.shape["col"]
    in_specs = (
        P(None, ("row", "col"), None),
        P(None, ("col", "row"), None),
        P(),
        P(),
        P("row", "col", None),
    )
    out_specs = (
        P("row", "col", None),
        P(None, ("row", "col"), None),
        P(None, ("col", "row"), None),
        P(),
        P(),
    )
    return jax.shard_map(
        functools.partial(per_device, nrow, ncol),
        mesh=mesh, in_specs=in_specs, out_specs=out_specs, check_vma=False,
    )
```

time: 332 us -> 92 us (0.28)
  matrix products: 101 us -> 0 us
  waiting for transfers between devices: 86.7 us -> 0 us
  Pallas kernels: 0 us -> 83.9 us
  blocking collectives: 50 us -> 0 us
  local copies, waits for them, and re-layouts: 49.2 us -> 7.17 us
  loops' own time: 23.5 us -> 0 us
  between operations: 14.5 us -> 0.67 us
  other arithmetic: 3.58 us -> 0 us
    dot_general x12 -> x0, matrix products: 101 us -> none  [the longest x2 33.9 us: visit(): jnp.einsum('ijcd,sic->sjd', grad_outer, left_block, precision=high)]
    psum x2 -> x0, waiting for transfers between devices: 86.7 us -> none  [the longest x1 52.6 us: per_device(): left_total = lax.psum(left_part, 'col')]
    pallas_call x0 -> x3, Pallas kernels: none -> 83.9 us  [the longest x1 46.5 us: per_device(): pl.pallas_call(functools.partial(reduce_kernel, nrow, ncol, tile_rows * n...]
    all_gather x2 -> x0, blocking collectives: 28.2 us -> none  [the longest x1 16.6 us: per_device(): left_all = lax.all_gather(left_factors, 'col', axis=1, tiled=True)]
    another operation x1 -> x0, loops' own time: 23.5 us -> none  [per_device(): lax.scan(visit, start, (left_blocks, cot_blocks))]
    psum x2 -> x0, blocking collectives: 21.9 us -> none  [the longest x1 11.8 us: per_device(): weight_total, bias_total = lax.psum((weight_half, bias_half), 'row')]
    dot_general x2 -> x0, local copies, waits for them, and re-layouts: 21.3 us -> none  [visit(): grad_flat = jnp.einsum('ije,ke->ijk', cot_block, weight, precision=high)]
    while x36 -> x0, local copies, waits for them, and re-layouts: 11.2 us -> none
  transfers between devices with their start and end apart: 2 -> 0, of which waited for: 2 -> 0; matrix products, arithmetic and copies ran while one was open for 1% -> 0% of each run, Pallas kernels for 0% -> 0%
where the time goes in v1:
time: 92 us; the launch traced here: 91.8 us
  Pallas kernels  83.9 us (91%)
  local copies, waits for them, and re-layouts  7.17 us (8%)
    pallas_call x1, Pallas kernels, per_device(): pl.pallas_call(functools.partial(reduce_kernel, nrow, ncol, tile_rows * n...  46.5 us
    pallas_call x1, Pallas kernels, per_device(): pl.pallas_call(functools.partial(compute_kernel, width), out_shape=(shape...  18.8 us
    pallas_call x1, Pallas kernels, per_device(): pl.pallas_call(functools.partial(gather_kernel, nrow, ncol), out_shape=(s...  18.7 us
    pallas_call x2, local copies, waits for them, and re-layouts, per_device(): pl.pallas_call(functools.partial(reduce_kernel, nrow, ncol, tile_rows * n...  2.42 us
    unnamed x8, local copies, waits for them, and re-layouts  2.39 us

profile of v1, /device:TPU:0, one launch (start us, length us, event | category | flops | bytes accessed | tf_op | source)
XLA Modules:
  0.0 91.8 jit_solution(8284815091754173481)
XLA Ops:
  0.6 0.0 copy-start
  0.6 1.6 %copy.15.r_ref = f32[128,128]{1,0:T(8,128)} copy(f32[128,128]{0,1:T(8,128)} %bitcast.13) | data formatting | bytes 131072 | tf_op jit(solution)/shard_map/reshape | solution.py:287
  2.2 0.0 copy-done
  2.2 0.8 copy.14.l_ref
  3.0 18.7 %gather.1 = (f32[4,128,256]{2,1,0:T(8,128)}, f32[8,128,128]{2,1,0:T(8,128)}) custom-call(f32[128,256]{1,0:T(8,128)} %copy.14.l_ref, f32[128,128]{1,0:T(8,128)} %copy.15.r_ref), custom_call_target="tpu_custom_call" | custom-call | tf_op jit(solution)/shard_map/gather/pallas_call | solution.py:279
  21.7 18.8 %tile.1 = (f32[1024,128]{1,0:T(8,128)}, f32[4,128,256]{2,1,0:T(8,128)}, f32[8,128,128]{2,1,0:T(8,128)}, f32[32,40,128]{2,1,0:T(8,128)}) custom-call(f32[4,128,256]{2,1,0:T(8,128)} %get-tuple-element.15.lo_ref, f32[8,128,128]{2,1,0:T(8,128)} %get-tuple-element.16.ro_ref, f32[1024,128]{1,0:T(8,128)} %w_ref.1, f32[1,128]{1,0:T(1,128)} %bitcast.15, ...), custom_call_target="tpu_custom_call" | custom-call | tf_op jit(solution)/shard_map/tile/pallas_call | solution.py:307
  40.5 46.5 %reduce.1 = (f32[128,256]{1,0:T(8,128)}, f32[128,128]{1,0:T(8,128)}, f32[32,32,128]{2,1,0:T(8,128)}, f32[1,128]{1,0:T(1,128)}) custom-call(f32[4,128,256]{2,1,0:T(8,128)} %get-tuple-element.18.lp_ref, f32[8,128,128]{2,1,0:T(8,128)} %get-tuple-element.19.rp_ref, f32[32,40,128]{2,1,0:T(8,128)} %get-tuple-element.20.wp_ref), custom_call_target="tpu_custom_call" | custom-call | tf_op jit(solution)/shard_map/reduce/pallas_call | solution.py:321
  87.0 0.0 copy-start.1
  87.0 1.7 %copy.16 = f32[128,256]{0,1:T(8,128)} copy(f32[128,256]{1,0:T(8,128)} %get-tuple-element.21) | data formatting | bytes 262144 | tf_op jit(solution)/shard_map/reduce/pallas_call | solution.py:321
  88.7 0.0 copy-done.1
  88.7 0.7 copy.17
  89.4 0.0 copy-start.2
  89.4 1.9 %copy.20 = f32[1024,128]{1,0:T(8,128)} copy(f32[1024,128]{1,0:T(8,128)} %bitcast.10) | data formatting | bytes 1048576
  91.3 0.0 copy-done.2
  91.3 0.5 copy.21
Async XLA Ops:
  0.6 1.6 %copy-start = (f32[128,8,32]{0,2,1:T(8,128)S(1)}, f32[128,8,32]{0,2,1:T(8,128)}, u32[]{:S(2)}) copy-start(f32[128,8,32]{0,2,1:T(8,128)} %param.5) | copy-start | bytes 393220
  87.0 1.7 %copy-start.1 = (f32[128,128]{1,0:T(8,128)S(1)}, f32[128,128]{1,0:T(8,128)}, u32[]{:S(2)}) copy-start(f32[128,128]{1,0:T(8,128)} %get-tuple-element.22) | copy-start | bytes 196612
  89.4 1.9 %copy-start.2 = (f32[1,128]{1,0:T(1,128)S(1)}, f32[1,128]{1,0:T(1,128)}, u32[]{:S(2)}) copy-start(f32[1,128]{1,0:T(1,128)} %get-tuple-element.24) | copy-start | bytes 1540

commit v2 on v0

v2 whole, which is shorter than its diff:
```python
import functools

import jax
import jax.numpy as jnp
from jax import lax
from jax.experimental import pallas as pl
from jax.experimental.pallas import tpu as pltpu
from jax.sharding import PartitionSpec as P

F32 = jnp.float32
BF16 = jnp.bfloat16
MESH = pl.DeviceIdType.MESH
VMEM = pl.BlockSpec(memory_space=pltpu.VMEM)
STEP = 8


def split(x):
    high = x.astype(BF16)
    return high, (x - high.astype(F32)).astype(BF16)


def dot(a, b):
    return lax.dot_general(a, b, (((1,), (0,)), ((), ())), preferred_element_type=F32)


def dot3(a_high, a_low, b_high, b_low):
    return dot(a_high, b_high) + (dot(a_high, b_low) + dot(a_low, b_high))


def swap_groups(pieces):
    lane = lax.broadcasted_iota(jnp.int32, pieces[0].shape, 1)
    low = lane < 64
    even = (lane & 32) == 0

    def far(a, b):
        moved = pltpu.roll(jnp.where(low, b, a), 64, 1)
        return jnp.where(low, a, moved), jnp.where(low, moved, b)

    def near(a, b):
        return (
            jnp.where(even, a, pltpu.roll(b, 32, 1)),
            jnp.where(even, pltpu.roll(a, 96, 1), b),
        )

    p0, p2 = far(pieces[0], pieces[2])
    p1, p3 = far(pieces[1], pieces[3])
    p0, p1 = near(p0, p1)
    p2, p3 = near(p2, p3)
    return p0, p1, p2, p3


def tile_kernel(
    nrow, ncol, width, l_ref, r_ref, w_ref, b_ref, cot_ref,
    pair_ref, lg_ref, rg_ref, wg_ref, bg_ref,
    lo, ro, lp, lbuf, rp, rbuf, wp, wbuf, part,
    l_h, l_l, lt_h, lt_l, r_h, r_l, rt_h, rt_l, w_h, w_l, wt_h, wt_l,
    c_h, c_l, ct_h, ct_l, h_h, h_l, o_scr, t_h, t_l, tmp,
    gls, glr, grs, grr, ls, lr, rs, rr, ws, wr, vs, vr, us, ur, xs, xr,
):
    row, col = lax.axis_index("row"), lax.axis_index("col")
    lw, samples = l_ref.shape
    rw = r_ref.shape[0]
    tile_rows, tile_cols = ncol * lw // width, nrow * rw // width
    channels, pair_width = w_ref.shape
    scale = 1.0 / samples
    per = 128 // width
    chunk = channels // nrow
    share = channels // (nrow * ncol)

    def in_row(peer):
        return {"row": peer, "col": col}

    def in_col(peer):
        return {"row": row, "col": peer}

    def block(ref, index, size):
        return ref.at[pl.ds(pl.multiple_of(index * size, size), size)]

    def each(count, here, act):
        @pl.loop(1, count)
        def _(k):
            act(lax.rem(here + k, count))

    def send(src, dst, send_sem, recv_sem, device):
        return pltpu.make_async_remote_copy(
            src_ref=src, dst_ref=dst, send_sem=send_sem, recv_sem=recv_sem,
            device_id=device, device_id_type=MESH,
        )

    def left_gather(peer, slot):
        return send(l_ref, block(lo, slot, lw), gls.at[peer], glr.at[slot], in_col(peer))

    def right_gather(peer, slot):
        return send(r_ref, block(ro, slot, rw), grs.at[peer], grr.at[slot], in_row(peer))

    def left_term(peer, slot):
        return send(block(lp, peer, lw), lbuf.at[slot], ls.at[peer], lr.at[slot], in_col(peer))

    def right_term(peer, slot):
        return send(block(rp, peer, rw), rbuf.at[slot], rs.at[peer], rr.at[slot], in_row(peer))

    def weight_row_term(peer, slot):
        return send(wp.at[peer], wbuf.at[slot], ws.at[peer], wr.at[slot], in_row(peer))

    def weight_col_term(peer, slot):
        return send(part.at[0, peer], part.at[1, slot], vs.at[peer], vr.at[slot], in_col(peer))

    def weight_col_whole(peer, slot):
        return send(wg_ref.at[row, col], wg_ref.at[row, slot], us.at[peer], ur.at[slot], in_col(peer))

    def weight_row_whole(peer, slot):
        return send(wg_ref.at[row], wg_ref.at[slot], xs.at[peer], xr.at[slot], in_row(peer))

    barrier = pltpu.get_barrier_semaphore()
    each(ncol, col, lambda p: pl.semaphore_signal(
        barrier, inc=1, device_id=in_col(p), device_id_type=MESH))
    each(nrow, row, lambda p: pl.semaphore_signal(
        barrier, inc=1, device_id=in_row(p), device_id_type=MESH))
    pl.semaphore_wait(barrier, nrow + ncol - 2)
    each(ncol, col, lambda p: left_gather(p, col).start())
    each(nrow, row, lambda p: right_gather(p, row).start())

    for d in range(width):
        tmp[d * width : (d + 1) * width, :] = w_ref[pl.ds(d, width, stride=width), :]
    weight = tmp[0:channels, :]
    w_h[...], w_l[...] = split(weight)
    wt_h[...], wt_l[...] = split(weight.T)
    cot = cot_ref[...]
    c_h[...], c_l[...] = split(cot)
    ct_h[...], ct_l[...] = split(cot.T)
    bias_tail = jnp.broadcast_to(jnp.sum(cot, axis=0, keepdims=True), (8, pair_width))
    pair_ref[...] = jnp.broadcast_to(b_ref[...], pair_ref.shape)

    step_lanes, step_rows = STEP * width, STEP * tile_cols
    halves = step_lanes // 128

    @pl.loop(0, tile_rows // STEP)
    def _(g):
        rows = pl.ds(pl.multiple_of(g * step_rows, step_rows), step_rows)
        grad = dot3(c_h[rows, :], c_l[rows, :], wt_h[...], wt_l[...]) * scale
        for b in range(width // per):
            for half in range(halves):
                pieces = [
                    grad[(half * per + a) * tile_cols : (half * per + a + 1) * tile_cols,
                         b * 128 : (b + 1) * 128]
                    for a in range(per)
                ]
                lanes = pl.ds(pl.multiple_of(g * step_lanes + half * 128, 128), 128)
                for a, piece in enumerate(swap_groups(pieces)):
                    at = (b * per + a) * tile_cols
                    high, low = split(piece)
                    h_h[at : at + tile_cols, lanes] = high
                    h_l[at : at + tile_cols, lanes] = low

    ro[pl.ds(pl.multiple_of(row * rw, rw), rw), :] = r_ref[...]
    each(nrow, row, lambda p: right_gather(p, p).wait())
    for d in range(width):
        tmp[d * tile_cols : (d + 1) * tile_cols, :] = ro[pl.ds(d, tile_cols, stride=width), :]
    right = tmp[0 : width * tile_cols, :]
    rt_h[...], rt_l[...] = split(right)
    r_h[...], r_l[...] = split(right.T)
    lo[pl.ds(pl.multiple_of(col * lw, lw), lw), :] = l_ref[...]
    each(ncol, col, lambda p: left_gather(p, p).wait())

    @pl.loop(0, tile_rows // STEP)
    def _(g):
        lanes = pl.ds(pl.multiple_of(g * step_lanes, step_lanes), step_lanes)
        lp[lanes, :] = dot3(r_h[...], r_l[...], h_h[:, lanes], h_l[:, lanes]).T

    each(ncol, col, lambda p: left_term(p, col).start())
    lbuf[col] = lp[pl.ds(pl.multiple_of(col * lw, lw), lw), :]
    left = lo[...]
    lt_h[...], lt_l[...] = split(left)
    l_h[...], l_l[...] = split(left.T)

    blocks = width // STEP
    block_rows, block_cols = STEP * tile_cols, STEP * width
    chunks = block_cols // chunk

    @pl.loop(0, blocks)
    def _(k):
        b = lax.rem(row // chunks + 1 + k, blocks)
        rows = pl.ds(pl.multiple_of(b * block_rows, block_rows), block_rows)
        cols = pl.ds(pl.multiple_of(b * block_cols, block_cols), block_cols)
        o_scr[...] = dot3(rt_h[rows, :], rt_l[rows, :], l_h[...], l_l[...]) * scale
        for q in range(STEP // per):
            for i in range(tile_rows // per):
                pieces = [
                    o_scr[(q * per + a) * tile_cols : (q * per + a + 1) * tile_cols,
                          i * 128 : (i + 1) * 128]
                    for a in range(per)
                ]
                for a, piece in enumerate(swap_groups(pieces)):
                    at = (i * per + a) * tile_cols
                    high, low = split(piece)
                    t_h[at : at + tile_cols, q * 128 : (q + 1) * 128] = high
                    t_l[at : at + tile_cols, q * 128 : (q + 1) * 128] = low
        terms = dot3(ct_h[...], ct_l[...], t_h[...], t_l[...]).T
        for m in range(chunks):
            peer = b * chunks + m
            wp[peer, 0:chunk, :] = terms[m * chunk : (m + 1) * chunk, :]
            wp[peer, chunk : chunk + 8, :] = bias_tail

            @pl.when(peer != row)
            def _():
                weight_row_term(peer, row).start()

        pair_ref[...] += dot3(t_h[...], t_l[...], w_h[cols, :], w_l[cols, :])

    for d in range(width):
        rows = slice(d * tile_cols, (d + 1) * tile_cols)
        rp[pl.ds(d, tile_cols, stride=width), :] = dot3(
            h_h[rows, :], h_l[rows, :], lt_h[...], lt_l[...]
        )
    each(nrow, row, lambda p: weight_row_term(p, p).wait())
    wbuf[row] = wp[row]
    total = functools.reduce(lambda a, b: a + b, [wbuf[q] for q in range(nrow)])
    for q in range(ncol):
        part[0, q, 0:share, :] = total[q * share : (q + 1) * share, :]
        part[0, q, share : share + 8, :] = total[chunk : chunk + 8, :]
    each(ncol, col, lambda p: weight_col_term(p, col).start())
    each(nrow, row, lambda p: right_term(p, row).start())
    rbuf[row] = rp[pl.ds(pl.multiple_of(row * rw, rw), rw), :]
    part[1, col] = part[0, col]
    each(ncol, col, lambda p: weight_col_term(p, p).wait())
    total = functools.reduce(lambda a, b: a + b, [part[1, q] for q in range(ncol)])
    total = total / (tile_rows * nrow)
    wg_ref[row, col] = total[0:share, :]
    bg_ref[...] = total[share : share + 1, :]
    each(ncol, col, lambda p: weight_col_whole(p, col).start())
    each(ncol, col, lambda p: left_term(p, p).wait())
    lg_ref[...] = functools.reduce(lambda a, b: a + b, [lbuf[q] for q in range(ncol)])
    each(ncol, col, lambda p: weight_col_whole(p, p).wait())
    each(nrow, row, lambda p: weight_row_whole(p, row).start())
    each(nrow, row, lambda p: right_term(p, p).wait())
    rg_ref[...] = functools.reduce(lambda a, b: a + b, [rbuf[q] for q in range(nrow)])
    each(nrow, row, lambda p: weight_row_whole(p, p).wait())


def per_device(nrow, ncol, left_factors, right_factors, weight, bias, cotangent):
    samples, li, width = left_factors.shape
    rj = right_factors.shape[1]
    tile_rows, tile_cols, pair_width = cotangent.shape
    channels = weight.shape[0]
    lw, rw = li * width, rj * width
    lefts, rights = tile_rows * width, tile_cols * width
    chunk, share = channels // nrow, channels // (nrow * ncol)
    dma = pltpu.SemaphoreType.DMA

    def shape(*dims):
        return jax.ShapeDtypeStruct(dims, F32)

    def two(*dims):
        return [pltpu.VMEM(dims, BF16)] * 2

    def buf(*dims):
        return pltpu.VMEM(dims, F32)

    scratch = [
        buf(lefts, samples), buf(rights, samples),
        buf(lefts, samples), buf(ncol, lw, samples),
        buf(rights, samples), buf(nrow, rw, samples),
        buf(nrow, chunk + 8, pair_width), buf(nrow, chunk + 8, pair_width),
        buf(2, ncol, share + 8, pair_width),
        *two(samples, lefts), *two(lefts, samples),
        *two(samples, rights), *two(rights, samples),
        *two(channels, pair_width), *two(pair_width, channels),
        *two(tile_rows * tile_cols, pair_width), *two(pair_width, tile_rows * tile_cols),
        *two(rights, lefts),
        buf(STEP * tile_cols, lefts), *two(tile_rows * tile_cols, STEP * width),
        buf(max(rights, channels), 128),
    ]
    for count in (ncol, nrow, ncol, nrow, nrow, ncol, ncol, nrow):
        scratch += [dma((count,)), dma((count,))]
    pair, lg, rg, wg, bg = pl.pallas_call(
        functools.partial(tile_kernel, nrow, ncol, width),
        out_shape=(
            shape(tile_rows * tile_cols, pair_width), shape(lw, samples), shape(rw, samples),
            shape(nrow, ncol, share, pair_width), shape(1, pair_width),
        ),
        in_specs=[VMEM] * 5,
        out_specs=[VMEM] * 5,
        scratch_shapes=scratch,
        compiler_params=pltpu.CompilerParams(collective_id=0, has_side_effects=True),
        name="tile",
    )(
        left_factors.transpose(1, 2, 0).reshape(lw, samples),
        right_factors.transpose(1, 2, 0).reshape(rw, samples),
        weight,
        bias.reshape(1, pair_width),
        cotangent.reshape(tile_rows * tile_cols, pair_width),
    )
    return (
        pair.reshape(tile_rows, tile_cols, pair_width),
        lg.reshape(li, width, samples).transpose(2, 0, 1),
        rg.reshape(rj, width, samples).transpose(2, 0, 1),
        wg.reshape(width, width, pair_width).transpose(1, 0, 2).reshape(channels, pair_width),
        bg.reshape(pair_width),
    )


def solution(mesh):
    nrow, ncol = mesh.shape["row"], mesh.shape["col"]
    in_specs = (
        P(None, ("row", "col"), None),
        P(None, ("col", "row"), None),
        P(),
        P(),
        P("row", "col", None),
    )
    out_specs = (
        P("row", "col", None),
        P(None, ("row", "col"), None),
        P(None, ("col", "row"), None),
        P(),
        P(),
    )
    return jax.shard_map(
        functools.partial(per_device, nrow, ncol),
        mesh=mesh, in_specs=in_specs, out_specs=out_specs, check_vma=False,
    )
```

time: 332 us -> 53.7 us (0.16)
  matrix products: 101 us -> 0 us
  waiting for transfers between devices: 86.7 us -> 0 us
  blocking collectives: 50 us -> 0 us
  Pallas kernels: 0 us -> 47.5 us
  local copies, waits for them, and re-layouts: 49.2 us -> 5.23 us
  loops' own time: 23.5 us -> 0 us
  between operations: 14.5 us -> 0.65 us
  other arithmetic: 3.58 us -> 0 us
    dot_general x12 -> x0, matrix products: 101 us -> none  [the longest x2 33.9 us: visit(): jnp.einsum('ijcd,sic->sjd', grad_outer, left_block, precision=high)]
    psum x2 -> x0, waiting for transfers between devices: 86.7 us -> none  [the longest x1 52.6 us: per_device(): left_total = lax.psum(left_part, 'col')]
    pallas_call x0 -> x1, Pallas kernels: none -> 47.5 us  [per_device(): pl.pallas_call(functools.partial(tile_kernel, nrow, ncol, width), out_sha...]
    all_gather x2 -> x0, blocking collectives: 28.2 us -> none  [the longest x1 16.6 us: per_device(): left_all = lax.all_gather(left_factors, 'col', axis=1, tiled=True)]
    another operation x1 -> x0, loops' own time: 23.5 us -> none  [per_device(): lax.scan(visit, start, (left_blocks, cot_blocks))]
    psum x2 -> x0, blocking collectives: 21.9 us -> none  [the longest x1 11.8 us: per_device(): weight_total, bias_total = lax.psum((weight_half, bias_half), 'row')]
    dot_general x2 -> x0, local copies, waits for them, and re-layouts: 21.3 us -> none  [visit(): grad_flat = jnp.einsum('ije,ke->ijk', cot_block, weight, precision=high)]
    reshape x2 -> x0, local copies, waits for them, and re-layouts: 13.4 us -> none  [visit(): flat = outer.reshape(step_rows, tile_cols, width * width)]
  transfers between devices with their start and end apart: 2 -> 0, of which waited for: 2 -> 0; matrix products, arithmetic and copies ran while one was open for 1% -> 0% of each run, Pallas kernels for 0% -> 0%
where the time goes in v2:
time: 53.7 us; the launch traced here: 53.4 us
  Pallas kernels  47.5 us (88%)
  local copies, waits for them, and re-layouts  5.23 us (10%)
  between operations  0.65 us (1%)
    pallas_call x1, Pallas kernels, per_device(): pl.pallas_call(functools.partial(tile_kernel, nrow, ncol, width), out_sha...  47.5 us
    unnamed x12, local copies, waits for them, and re-layouts  3.03 us
    transpose x1, local copies, waits for them, and re-layouts, per_device(): wg.reshape(width, width, pair_width).transpose(1, 0, 2)  2.2 us

profile of v2, /device:TPU:0, one launch (start us, length us, event | category | flops | bytes accessed | tf_op | source)
XLA Modules:
  0.0 53.4 jit_solution(9084866092937691257)
XLA Ops:
  0.6 47.5 %tile.1 = (f32[1024,128]{1,0:T(8,128)}, f32[256,128]{1,0:T(8,128)}, f32[128,128]{1,0:T(8,128)}, f32[8,4,32,128]{3,2,1,0:T(8,128)}, f32[1,128]{1,0:T(1,128)}) custom-call(f32[256,128]{1,0:T(8,128)} %bitcast.24, f32[128,128]{1,0:T(8,128)} %bitcast.26, f32[1024,128]{1,0:T(8,128)} %w_ref.1, f32[1,128]{1,0:T(1,128)} %bitcast.28, f32[1024,128]{1,0:T(8,128)} %bitcast.20), custom_call_target="tpu_custom_call" | custom-call | tf_op jit(solution)/shard_map/tile/pallas_call | solution.py:275
  48.2 0.0 copy-start
  48.2 2.2 %copy.10 = f32[32,32,128]{2,1,0:T(8,128)} copy(f32[32,32,128]{2,0,1:T(8,128)} %bitcast.23) | data formatting | bytes 1048576 | tf_op jit(solution)/shard_map/transpose | solution.py:297
  50.4 0.0 copy-done
  50.4 0.0 copy-start.1
  50.4 0.8 %copy.15 = f32[32,32,128]{2,1,0:T(8,128)} copy(f32[32,32,128]{2,1,0:T(8,128)S(1)} %bitcast.22) | data formatting | bytes 1048576
  51.2 0.2 copy-done.1
  51.4 0.0 copy-start.2
  51.4 0.7 %copy.16 = f32[128,8,32]{0,2,1:T(8,128)} copy(f32[128,8,32]{0,2,1:T(8,128)S(1)} %bitcast.25) | data formatting | bytes 262144
  52.1 0.2 copy-done.2
  52.3 0.0 copy-start.3
  52.3 0.6 %copy.17 = f32[128,4,32]{0,2,1:T(8,128)} copy(f32[128,4,32]{0,2,1:T(8,128)S(1)} %bitcast.27) | data formatting | bytes 131072
  52.9 0.0 copy-done.3
  52.9 0.5 copy.18
Async XLA Ops:
  48.2 2.2 %copy-start = (f32[1024,128]{1,0:T(8,128)S(1)}, f32[1024,128]{1,0:T(8,128)}, u32[]{:S(2)}) copy-start(f32[1024,128]{1,0:T(8,128)} %get-tuple-element.10) | copy-start | bytes 1572868
  50.4 1.0 %copy-start.1 = (f32[256,128]{1,0:T(8,128)S(1)}, f32[256,128]{1,0:T(8,128)}, u32[]{:S(2)}) copy-start(f32[256,128]{1,0:T(8,128)} %get-tuple-element.11) | copy-start | bytes 393220
  51.4 0.9 %copy-start.2 = (f32[128,128]{1,0:T(8,128)S(1)}, f32[128,128]{1,0:T(8,128)}, u32[]{:S(2)}) copy-start(f32[128,128]{1,0:T(8,128)} %get-tuple-element.12) | copy-start | bytes 196612
  52.3 0.6 %copy-start.3 = (f32[1,128]{1,0:T(1,128)S(1)}, f32[1,128]{1,0:T(1,128)}, u32[]{:S(2)}) copy-start(f32[1,128]{1,0:T(1,128)} %get-tuple-element.14) | copy-start | bytes 1540

commit v3 on v2

--- a/solution.py
+++ b/solution.py
@@ -27,6 +27,12 @@
     return dot(a_high, b_high) + (dot(a_high, b_low) + dot(a_low, b_high))
 
 
+def dot_wide(a_high, a_low, b_both):
+    half = b_both.shape[1] // 2
+    wide = dot(a_high, b_both)
+    return wide[:, 0:half] + (wide[:, half:] + dot(a_low, b_both[:, 0:half]))
+
+
 def swap_groups(pieces):
     lane = lax.broadcasted_iota(jnp.int32, pieces[0].shape, 1)
     low = lane < 64
@@ -53,9 +59,9 @@
     nrow, ncol, width, l_ref, r_ref, w_ref, b_ref, cot_ref,
     pair_ref, lg_ref, rg_ref, wg_ref, bg_ref,
     lo, ro, lp, lbuf, rp, rbuf, wp, wbuf, part,
-    l_h, l_l, lt_h, lt_l, r_h, r_l, rt_h, rt_l, w_h, w_l, wt_h, wt_l,
+    l_c, l_l, lt_c, r_h, r_l, rt_c, w_c, wt_h, wt_l,
     c_h, c_l, ct_h, ct_l, h_h, h_l, o_scr, t_h, t_l, tmp,
-    gls, glr, grs, grr, ls, lr, rs, rr, ws, wr, vs, vr, us, ur, xs, xr,
+    gls, glr, grs, grr, ls, lr, rs, rr, ws, wr, vs, vr, us, ur, xs, xr, fs, fr,
 ):
     row, col = lax.axis_index("row"), lax.axis_index("col")
     lw, samples = l_ref.shape
@@ -111,6 +117,16 @@
     def weight_row_whole(peer, slot):
         return send(wg_ref.at[row], wg_ref.at[slot], xs.at[peer], xr.at[slot], in_row(peer))
 
+    partner = row + 1 - 2 * lax.rem(row, 2)
+
+    def weight_pass(index):
+        return send(wg_ref.at[index], wg_ref.at[index], fs.at[index], fr.at[index], in_row(partner))
+
+    def same_core(act):
+        @pl.loop(1, nrow // 2)
+        def _(k):
+            act(lax.rem(row + 2 * k, nrow))
+
     barrier = pltpu.get_barrier_semaphore()
     each(ncol, col, lambda p: pl.semaphore_signal(
         barrier, inc=1, device_id=in_col(p), device_id_type=MESH))
@@ -123,7 +139,7 @@
     for d in range(width):
         tmp[d * width : (d + 1) * width, :] = w_ref[pl.ds(d, width, stride=width), :]
     weight = tmp[0:channels, :]
-    w_h[...], w_l[...] = split(weight)
+    w_c[:, 0:pair_width], w_c[:, pair_width:] = split(weight)
     wt_h[...], wt_l[...] = split(weight.T)
     cot = cot_ref[...]
     c_h[...], c_l[...] = split(cot)
@@ -157,7 +173,7 @@
     for d in range(width):
         tmp[d * tile_cols : (d + 1) * tile_cols, :] = ro[pl.ds(d, tile_cols, stride=width), :]
     right = tmp[0 : width * tile_cols, :]
-    rt_h[...], rt_l[...] = split(right)
+    rt_c[:, 0:samples], rt_c[:, samples:] = split(right)
     r_h[...], r_l[...] = split(right.T)
     lo[pl.ds(pl.multiple_of(col * lw, lw), lw), :] = l_ref[...]
     each(ncol, col, lambda p: left_gather(p, p).wait())
@@ -170,8 +186,10 @@
     each(ncol, col, lambda p: left_term(p, col).start())
     lbuf[col] = lp[pl.ds(pl.multiple_of(col * lw, lw), lw), :]
     left = lo[...]
-    lt_h[...], lt_l[...] = split(left)
-    l_h[...], l_l[...] = split(left.T)
+    lt_c[:, 0:samples], lt_c[:, samples:] = split(left)
+    high, l_l[...] = split(left.T)
+    l_c[0:samples, :] = high
+    l_c[samples:, :] = high
 
     blocks = width // STEP
     block_rows, block_cols = STEP * tile_cols, STEP * width
@@ -182,7 +200,9 @@
         b = lax.rem(row // chunks + 1 + k, blocks)
         rows = pl.ds(pl.multiple_of(b * block_rows, block_rows), block_rows)
         cols = pl.ds(pl.multiple_of(b * block_cols, block_cols), block_cols)
-        o_scr[...] = dot3(rt_h[rows, :], rt_l[rows, :], l_h[...], l_l[...]) * scale
+        o_scr[...] = (
+            dot(rt_c[rows, :], l_c[...]) + dot(rt_c[rows, 0:samples], l_l[...])
+        ) * scale
         for q in range(STEP // per):
             for i in range(tile_rows // per):
                 pieces = [
@@ -205,13 +225,11 @@
             def _():
                 weight_row_term(peer, row).start()
 
-        pair_ref[...] += dot3(t_h[...], t_l[...], w_h[cols, :], w_l[cols, :])
+        pair_ref[...] += dot_wide(t_h[...], t_l[...], w_c[cols, :])
 
     for d in range(width):
         rows = slice(d * tile_cols, (d + 1) * tile_cols)
-        rp[pl.ds(d, tile_cols, stride=width), :] = dot3(
-            h_h[rows, :], h_l[rows, :], lt_h[...], lt_l[...]
-        )
+        rp[pl.ds(d, tile_cols, stride=width), :] = dot_wide(h_h[rows, :], h_l[rows, :], lt_c[...])
     each(nrow, row, lambda p: weight_row_term(p, p).wait())
     wbuf[row] = wp[row]
     total = functools.reduce(lambda a, b: a + b, [wbuf[q] for q in range(nrow)])
@@ -231,10 +249,44 @@
     each(ncol, col, lambda p: left_term(p, p).wait())
     lg_ref[...] = functools.reduce(lambda a, b: a + b, [lbuf[q] for q in range(ncol)])
     each(ncol, col, lambda p: weight_col_whole(p, p).wait())
-    each(nrow, row, lambda p: weight_row_whole(p, row).start())
+    weight_pass(row).start()
+    same_core(lambda p: weight_row_whole(p, row).start())
+
+    def pass_on(p):
+        weight_row_whole(p, p).wait_recv()
+        weight_pass(p).start()
+
+    same_core(pass_on)
     each(nrow, row, lambda p: right_term(p, p).wait())
     rg_ref[...] = functools.reduce(lambda a, b: a + b, [rbuf[q] for q in range(nrow)])
-    each(nrow, row, lambda p: weight_row_whole(p, p).wait())
+    same_core(lambda p: weight_row_whole(p, p).wait_send())
+
+    @pl.loop(0, nrow // 2)
+    def _(k):
+        weight_pass(lax.rem(row + 2 * k, nrow)).wait_send()
+        weight_pass(lax.rem(partner + 2 * k, nrow)).wait_recv()
+
+
+def finish_kernel(
+    width, pair_ref, lg_ref, rg_ref, wg_ref, bg_ref,
+    pair_out, lg_out, rg_out, w_out, bg_out, held, sems,
+):
+    copies = [
+        pltpu.make_async_copy(src, dst, sems.at[k])
+        for k, (src, dst) in enumerate([
+            (wg_ref, held), (pair_ref, pair_out), (lg_ref, lg_out), (rg_ref, rg_out), (bg_ref, bg_out),
+        ])
+    ]
+    for copy in copies:
+        copy.start()
+    copies[0].wait()
+    nrow, ncol, share, _ = held.shape
+    for r in range(nrow):
+        for q in range(ncol):
+            d, c = divmod((r * ncol + q) * share, width)
+            w_out[pl.ds(c * width + d, share, stride=width), :] = held[r, q]
+    for copy in copies[1:]:
+        copy.wait()
 
 
 def per_device(nrow, ncol, left_factors, right_factors, weight, bias, cotangent):
@@ -262,15 +314,16 @@
         buf(rights, samples), buf(nrow, rw, samples),
         buf(nrow, chunk + 8, pair_width), buf(nrow, chunk + 8, pair_width),
         buf(2, ncol, share + 8, pair_width),
-        *two(samples, lefts), *two(lefts, samples),
-        *two(samples, rights), *two(rights, samples),
-        *two(channels, pair_width), *two(pair_width, channels),
+        pltpu.VMEM((2 * samples, lefts), BF16), pltpu.VMEM((samples, lefts), BF16),
+        pltpu.VMEM((lefts, 2 * samples), BF16),
+        *two(samples, rights), pltpu.VMEM((rights, 2 * samples), BF16),
+        pltpu.VMEM((channels, 2 * pair_width), BF16), *two(pair_width, channels),
         *two(tile_rows * tile_cols, pair_width), *two(pair_width, tile_rows * tile_cols),
         *two(rights, lefts),
         buf(STEP * tile_cols, lefts), *two(tile_rows * tile_cols, STEP * width),
         buf(max(rights, channels), 128),
     ]
-    for count in (ncol, nrow, ncol, nrow, nrow, ncol, ncol, nrow):
+    for count in (ncol, nrow, ncol, nrow, nrow, ncol, ncol, nrow, nrow):
         scratch += [dma((count,)), dma((count,))]
     pair, lg, rg, wg, bg = pl.pallas_call(
         functools.partial(tile_kernel, nrow, ncol, width),
@@ -290,11 +343,23 @@
         bias.reshape(1, pair_width),
         cotangent.reshape(tile_rows * tile_cols, pair_width),
     )
+    whole = pl.BlockSpec(memory_space=pl.ANY)
+    pair, lg, rg, wg, bg = pl.pallas_call(
+        functools.partial(finish_kernel, width),
+        out_shape=(
+            shape(tile_rows * tile_cols, pair_width), shape(lw, samples), shape(rw, samples),
+            shape(channels, pair_width), shape(1, pair_width),
+        ),
+        in_specs=[whole] * 5,
+        out_specs=[VMEM] * 5,
+        scratch_shapes=[buf(nrow, ncol, share, pair_width), dma((5,))],
+        name="finish",
+    )(pair, lg, rg, wg, bg)
     return (
         pair.reshape(tile_rows, tile_cols, pair_width),
         lg.reshape(li, width, samples).transpose(2, 0, 1),
         rg.reshape(rj, width, samples).transpose(2, 0, 1),
-        wg.reshape(width, width, pair_width).transpose(1, 0, 2).reshape(channels, pair_width),
+        wg,
         bg.reshape(pair_width),
     )
 

time: 53.7 us -> 51 us (0.950)
  local copies, waits for them, and re-layouts: 5.23 us -> 0 us
  Pallas kernels: 47.5 us -> 50.2 us
    unnamed x12 -> x0, local copies, waits for them, and re-layouts: 3.03 us -> none
    pallas_call x0 -> x1, Pallas kernels: none -> 2.61 us  [per_device(): pl.pallas_call(functools.partial(finish_kernel, width), out_shape=(shape(...]
    transpose x1 -> x0, local copies, waits for them, and re-layouts: 2.2 us -> none  [per_device(): wg.reshape(width, width, pair_width).transpose(1, 0, 2)]
where the time goes in v3:
time: 51 us; the launch traced here: 50.8 us
  Pallas kernels  50.2 us (98%)
  between operations  0.64 us (1%)
    pallas_call x1, Pallas kernels, per_device(): pl.pallas_call(functools.partial(tile_kernel, nrow, ncol, width), out_sha...  47.5 us
    pallas_call x1, Pallas kernels, per_device(): pl.pallas_call(functools.partial(finish_kernel, width), out_shape=(shape(...  2.61 us

profile of v3, /device:TPU:0, one launch (start us, length us, event | category | flops | bytes accessed | tf_op | source)
XLA Modules:
  0.0 50.8 jit_solution(1193147472264510408)
XLA Ops:
  0.6 47.5 %tile.1 = (f32[1024,128]{1,0:T(8,128)}, f32[256,128]{1,0:T(8,128)}, f32[128,128]{1,0:T(8,128)}, f32[8,4,32,128]{3,2,1,0:T(8,128)}, f32[1,128]{1,0:T(1,128)}) custom-call(f32[256,128]{1,0:T(8,128)} %bitcast.17, f32[128,128]{1,0:T(8,128)} %bitcast.18, f32[1024,128]{1,0:T(8,128)} %w_ref.1, f32[1,128]{1,0:T(1,128)} %bitcast.19, f32[1024,128]{1,0:T(8,128)} %bitcast.16), custom_call_target="tpu_custom_call" | custom-call | tf_op jit(solution)/shard_map/tile/pallas_call | solution.py:328
  48.2 2.6 %finish.1 = (f32[1024,128]{1,0:T(8,128)}, f32[256,128]{1,0:T(8,128)}, f32[128,128]{1,0:T(8,128)}, f32[1024,128]{1,0:T(8,128)}, f32[1,128]{1,0:T(1,128)}) custom-call(f32[1024,128]{1,0:T(8,128)} %get-tuple-element.15.pair_ref, f32[256,128]{1,0:T(8,128)} %get-tuple-element.16.lg_ref, f32[128,128]{1,0:T(8,128)} %get-tuple-element.17.rg_ref, ...), custom_call_target="tpu_custom_call" | custom-call | tf_op jit(solution)/shard_map/finish/pallas_call | solution.py:347

commit v4 on v3

--- a/solution.py
+++ b/solution.py
@@ -246,11 +246,12 @@
     wg_ref[row, col] = total[0:share, :]
     bg_ref[...] = total[share : share + 1, :]
     each(ncol, col, lambda p: weight_col_whole(p, col).start())
-    each(ncol, col, lambda p: left_term(p, p).wait())
-    lg_ref[...] = functools.reduce(lambda a, b: a + b, [lbuf[q] for q in range(ncol)])
     each(ncol, col, lambda p: weight_col_whole(p, p).wait())
     weight_pass(row).start()
     same_core(lambda p: weight_row_whole(p, row).start())
+
+    each(ncol, col, lambda p: left_term(p, p).wait())
+    lg_ref[...] = functools.reduce(lambda a, b: a + b, [lbuf[q] for q in range(ncol)])
 
     def pass_on(p):
         weight_row_whole(p, p).wait_recv()

time: 51 us -> 51 us (level)
  no operation moved by 1% of the time
where the time goes in v4:
time: 51 us; the launch traced here: 50.8 us
  Pallas kernels  50.2 us (98%)
  between operations  0.64 us (1%)
    pallas_call x1, Pallas kernels, per_device(): pl.pallas_call(functools.partial(tile_kernel, nrow, ncol, width), out_sha...  47.5 us
    pallas_call x1, Pallas kernels, per_device(): pl.pallas_call(functools.partial(finish_kernel, width), out_shape=(shape(...  2.61 us

profile of v4, /device:TPU:0, one launch (start us, length us, event | category | flops | bytes accessed | tf_op | source)
XLA Modules:
  0.0 50.8 jit_solution(16862738336949156306)
XLA Ops:
  0.6 47.5 %tile.1 = (f32[1024,128]{1,0:T(8,128)}, f32[256,128]{1,0:T(8,128)}, f32[128,128]{1,0:T(8,128)}, f32[8,4,32,128]{3,2,1,0:T(8,128)}, f32[1,128]{1,0:T(1,128)}) custom-call(f32[256,128]{1,0:T(8,128)} %bitcast.17, f32[128,128]{1,0:T(8,128)} %bitcast.18, f32[1024,128]{1,0:T(8,128)} %w_ref.1, f32[1,128]{1,0:T(1,128)} %bitcast.19, f32[1024,128]{1,0:T(8,128)} %bitcast.16), custom_call_target="tpu_custom_call" | custom-call | tf_op jit(solution)/shard_map/tile/pallas_call | solution.py:329
  48.2 2.6 %finish.1 = (f32[1024,128]{1,0:T(8,128)}, f32[256,128]{1,0:T(8,128)}, f32[128,128]{1,0:T(8,128)}, f32[1024,128]{1,0:T(8,128)}, f32[1,128]{1,0:T(1,128)}) custom-call(f32[1024,128]{1,0:T(8,128)} %get-tuple-element.15.pair_ref, f32[256,128]{1,0:T(8,128)} %get-tuple-element.16.lg_ref, f32[128,128]{1,0:T(8,128)} %get-tuple-element.17.rg_ref, ...), custom_call_target="tpu_custom_call" | custom-call | tf_op jit(solution)/shard_map/finish/pallas_call | solution.py:348
